TPU v7x, 512 devices: a whole 4x8x8 slice. The times are simulated.
512 devices in a mesh: aux: 32 (over x_lo, y, core), pair: 16 (over z, x_hi).
Axes of the slice: x: 4 (x_hi: 2, x_lo: 2; x = x_hi * 2 + x_lo), y: 8, z: 8, core: 2. Of those that a mesh axis runs over, the one named last changes fastest.
Arguments:
- integrals: bfloat16 [4096, 32, 512], P('aux', 'pair'), may hold values from -0.5 to 0.5
- occ_density: bfloat16 [32, 32], replicated, may hold values from -1 to 1
- virt_density: bfloat16 [512, 512], replicated, may hold values from -0.25 to 0.25
- screen: int32 [64, 32], P('aux', 'pair'), may hold values 0 or 1
Outputs:
- polar: float32 [4096, 4096], P('aux', 'pair')
All inputs are finite; a program needn't handle non-finite values. No bound on the sum of `screen` on one device may be relied on, other than what follows from the above.
Results may differ from a plain program's by a relative error of at most 0.0041.
Values may be sent and summed in bfloat16 or wider, within the bound.
No kernel may reach another device: no remote copies, remote signals or barrier semaphores. Data moves between devices by JAX's collectives and lax.ppermute only.
A program may use at most 64 MiB of HBM per device.

v0:
```python
import jax
import jax.numpy as jnp
from jax import lax
from jax.sharding import Mesh, PartitionSpec as P

AUX = ("x_lo", "y", "core")
PAIR = ("z", "x_hi")
PLANE = ("x_lo", "core", "z", "x_hi")
WIDE = ("x_lo", "core", "x_hi")


def exchange(values):
    pieces = values.reshape(2, 2, 2, 16, 2, 8, 64)
    pieces = pieces.transpose(0, 1, 5, 2, 3, 4, 6).reshape(64, 16, 128)
    got = lax.all_to_all(pieces, PLANE, 0, 0, tiled=True)
    got = got.reshape(4, 16, 16, 128).transpose(0, 2, 1, 3)
    return got.reshape(64, 2048)


def body(integrals, occ_density, virt_density, screen):
    aux_rows, local_pairs, orbitals = integrals.shape
    blocks = screen.shape[0]
    grouped = integrals.reshape(blocks, aux_rows // blocks, local_pairs, orbitals)
    screened = jnp.where(screen[:, None, :, None] > 0, grouped, jnp.zeros_like(grouped)).reshape(
        aux_rows, local_pairs, orbitals
    )
    virtual = (
        jnp.dot(
            screened.reshape(aux_rows * local_pairs, orbitals),
            virt_density,
            preferred_element_type=jnp.float32,
        )
        .astype(jnp.bfloat16)
        .reshape(aux_rows, local_pairs, orbitals)
    )
    mine = exchange(screened)
    columns = lax.all_gather(mine, "y", axis=0, tiled=True)
    virt_rows = exchange(virtual).reshape(64, 32, 64)
    occupied = jnp.einsum("pms,ml->pls", virt_rows, occ_density, preferred_element_type=jnp.float32)
    occupied = occupied.astype(jnp.bfloat16).reshape(64, 2048)
    rows = lax.all_gather(occupied, WIDE, axis=0, tiled=True)
    rows = rows.reshape(8, 4, 16, 2048).transpose(1, 0, 2, 3).reshape(512, 2048)
    part = lax.dot_general(
        columns, rows, (((1,), (1,)), ((), ())), preferred_element_type=jnp.float32
    )
    part = part.astype(jnp.bfloat16)
    tiles = part.reshape(4, 2, 2, 32, 2, 2, 128).transpose(4, 5, 2, 0, 1, 3, 6).reshape(64, 32, 128)
    got = lax.all_to_all(tiles, PLANE, 0, 0, tiled=True)
    total = jnp.sum(got.reshape(2, 2, 8, 2, 2, 16, 128).astype(jnp.float32), axis=2)
    return total.transpose(5, 3, 0, 1, 2, 4).reshape(128, 256)


def solution(mesh):
    fine = Mesh(mesh.devices.reshape(2, 8, 2, 8, 2), AUX + PAIR)
    placed = (P(AUX, PAIR, None), P(), P(), P(AUX, PAIR))
    return jax.shard_map(body, mesh=fine, in_specs=placed, out_specs=P(AUX, PAIR), check_vma=False)
```

profile of v0, /device:TPU:6, one launch (start us, length us, event | category | flops | bytes accessed | tf_op | source)
XLA Modules:
  0.0 188.4 jit_solution(10271872201832409334)
XLA Ops:
  6.5 0.7 broadcast_compare_fusion
  7.3 0.1 broadcast_in_dim.23
  7.4 1.1 reshape.50
  8.5 0.3 convolution_convert_fusion.2
  8.9 0.0 copy-start.2
  8.9 0.3 reshape_reshape.8
  9.2 0.5 copy.36
  9.7 0.3 reshape.51
  10.0 0.0 copy-start.1
  10.0 26.7 %all_to_all.15 = bf16[64,16,128]{2,1,0:T(8,128)(2,1)S(1)} all-to-all(bf16[64,16,128]{2,1,0:T(8,128)(2,1)S(1)} %reshape.51), channel_id=1, replica_groups=mesh['x_lo'=2,'y'=8,'core'=2,'z'=8,'x_hi'=2] {'x_lo','core','z','x_hi'}, dimensions={0} | all-to-all | bytes 524288 | tf_op jit(solution)/shard_map/all_to_all | solution.py:15
  36.7 0.1 copy.24
  36.7 0.2 reshape_reshape.9
  37.0 0.3 fusion
  37.3 1.2 reshape.53
  38.5 0.0 all-gather.5.cloned.1.call-update
  38.6 0.0 all-gather.3.cloned.1.call-start
  38.6 0.3 reshape.46
  39.0 0.6 fusion.1
  39.5 0.3 reshape.47
  39.8 17.9 %all_to_all.16 = bf16[64,16,128]{2,1,0:T(8,128)(2,1)S(1)} all-to-all(bf16[64,16,128]{2,1,0:T(8,128)(2,1)S(1)} %reshape.47), channel_id=1, replica_groups=mesh['x_lo'=2,'y'=8,'core'=2,'z'=8,'x_hi'=2] {'x_lo','core','z','x_hi'}, dimensions={0} | all-to-all | bytes 524288 | tf_op jit(solution)/shard_map/all_to_all | solution.py:15
  57.8 0.1 copy.22
  57.8 0.8 copy.37
  58.6 0.0 all-gather.3.cloned.1.call-update
  58.6 36.2 %all-gather.5.cloned.1.call-done = bf16[512,2048]{1,0:T(8,128)(2,1)} async-done(((bf16[64,2048]{1,0:T(8,128)(2,1)}), bf16[512,2048]{1,0:T(8,128)(2,1)}) %all-gather.5.cloned.1.call-update) | async-done | bytes 2097168 | tf_op jit(solution)/shard_map/all_gather | solution.py:41
  94.9 1.7 copy.26
  96.6 51.8 %all-gather.3.cloned.1.call-done = bf16[512,2048]{1,0:T(8,128)(2,1)} async-done(((bf16[64,2048]{1,0:T(8,128)(2,1)}), bf16[512,2048]{1,0:T(8,128)(2,1)}) %all-gather.3.cloned.1.call-update) | async-done | bytes 2097168 | tf_op jit(solution)/shard_map/all_gather | solution.py:37
  148.4 2.9 %convolution_convert_fusion = bf16[512,512]{1,0:T(8,128)(2,1)S(1)} fusion(bf16[512,2048]{1,0:T(8,128)(2,1)} %all-gather.3.cloned.1.call-done, bf16[512,2048]{1,0:T(8,128)(2,1)S(1)} %bitcast.39), kind=kOutput, calls=%fused_computation | convolution fusion | flops 1074003968 | bytes 4718592 | tf_op jit(solution)/shard_map/dot_general | solution.py:43
  151.2 0.1 reshape.56
  151.4 0.1 copy.27
  151.5 29.3 %all_to_all.17 = bf16[64,32,128]{2,1,0:T(8,128)(2,1)S(1)} all-to-all(bf16[64,32,128]{2,1,0:T(8,128)(2,1)S(1)} %bitcast.41), channel_id=1, replica_groups=mesh['x_lo'=2,'y'=8,'core'=2,'z'=8,'x_hi'=2] {'x_lo','core','z','x_hi'}, dimensions={0} | all-to-all | bytes 1048576 | tf_op jit(solution)/shard_map/all_to_all | solution.py:48
  180.7 0.1 convert_reduce_fusion
  180.8 0.8 copy.29
  (7 shorter events, 0.0 us)
Async XLA Ops:
  6.5 2.0 %copy-start = (bf16[512,512]{1,0:T(8,128)(2,1)S(1)}, bf16[512,512]{1,0:T(8,128)(2,1)}, u32[]{:S(2)}) copy-start(bf16[512,512]{1,0:T(8,128)(2,1)} %param.6) | copy-start | bytes 1572868
  6.5 88.3 %all-gather.5.cloned.1.call-start = ((), (), s32[]{:S(2)}) async-start(), calls=%async_computation.4 | async-start | bytes 2359296 | tf_op jit(solution)/shard_map/all_gather | solution.py:41
  8.9 28.1 %copy-start.2 = (bf16[32,32]{1,0:T(8,128)(2,1)S(1)}, bf16[32,32]{1,0:T(8,128)(2,1)}, u32[]{:S(2)}) copy-start(bf16[32,32]{1,0:T(8,128)(2,1)} %param.5) | copy-start | bytes 6148
  10.0 28.6 %copy-start.1 = (bf16[128,2,512]{2,1,0:T(2,128)(2,1)S(1)}, bf16[128,2,512]{2,1,0:T(2,128)(2,1)}, u32[]{:S(2)}) copy-start(bf16[128,2,512]{2,1,0:T(2,128)(2,1)} %param.4) | copy-start | bytes 786436
  38.6 109.8 %all-gather.3.cloned.1.call-start = ((), (), s32[]{:S(2)}) async-start(), calls=%async_computation.3 | async-start | bytes 2359296 | tf_op jit(solution)/shard_map/all_gather | solution.py:37
Sparse Core Ops, SparseCore 0:
  38.7 56.1 all-gather.4
  96.9 51.3 all-gather.2
where the time goes:
time: 189 us; the launch traced here: 188 us
  waiting for transfers between devices  88 us (47%)
  blocking collectives  73.9 us (39%)
  between operations  13.6 us (7%)
  local copies, waits for them, and re-layouts  7.99 us (4%)
  matrix products  3.54 us (2%)
    all_gather x1, waiting for transfers between devices, body(): columns = lax.all_gather(mine, 'y', axis=0, tiled=True)  51.8 us
    all_to_all x2, blocking collectives, exchange(): got = lax.all_to_all(pieces, PLANE, 0, 0, tiled=True)  44.6 us
    all_gather x1, waiting for transfers between devices, body(): rows = lax.all_gather(occupied, WIDE, axis=0, tiled=True)  36.2 us
    all_to_all x1, blocking collectives, body(): got = lax.all_to_all(tiles, PLANE, 0, 0, tiled=True)  29.3 us
  transfers between devices with their start and end apart: 2, of which 2 were waited for; matrix products, arithmetic and copies ran while one was open for 2% of the time, Pallas kernels for 0%

commit v1 on v0

--- a/solution.py
+++ b/solution.py
@@ -34,7 +34,8 @@
         .reshape(aux_rows, local_pairs, orbitals)
     )
     mine = exchange(screened)
-    columns = lax.all_gather(mine, "y", axis=0, tiled=True)
+    sent = jnp.stack([mine] * lax.axis_size("y"))
+    columns = jnp.concatenate(lax.all_to_all(sent, "y", 0, 0), axis=0)
     virt_rows = exchange(virtual).reshape(64, 32, 64)
     occupied = jnp.einsum("pms,ml->pls", virt_rows, occ_density, preferred_element_type=jnp.float32)
     occupied = occupied.astype(jnp.bfloat16).reshape(64, 2048)

time: 189 us -> 162 us (0.86)
  blocking collectives: 73.9 us -> 34 us
  starting transfers between devices: 0.04 us -> 26.6 us
  waiting for transfers between devices: 88 us -> 70.5 us
  local copies, waits for them, and re-layouts: 7.99 us -> 11.7 us
    all_gather x1 -> x0, waiting for transfers between devices: 51.8 us -> none  [body(): columns = lax.all_gather(mine, 'y', axis=0, tiled=True)]
    all_to_all x2 -> x0, blocking collectives: 44.6 us -> none  [exchange(): got = lax.all_to_all(pieces, PLANE, 0, 0, tiled=True)]
    all_to_all x0 -> x3, starting transfers between devices: none -> 26.5 us  [the longest x2 19.4 us: exchange(): got = lax.all_to_all(pieces, PLANE, 0, 0, tiled=True)]
    all_to_all x0 -> x3, waiting for transfers between devices: none -> 23 us  [the longest x2 23 us: exchange(): got = lax.all_to_all(pieces, PLANE, 0, 0, tiled=True)]
    all_gather x1, waiting for transfers between devices: 36.2 us -> 47.4 us  [body(): rows = lax.all_gather(occupied, WIDE, axis=0, tiled=True)]
    all_to_all x1, blocking collectives: 29.3 us -> 34 us  [body(): got = lax.all_to_all(tiles, PLANE, 0, 0, tiled=True)]
  transfers between devices with their start and end apart: 2 -> 4, of which waited for: 2 -> 3; matrix products, arithmetic and copies ran while one was open for 2% -> 4% of each run, Pallas kernels for 0% -> 0%
where the time goes in v1:
time: 162 us; the launch traced here: 161 us
  waiting for transfers between devices  70.5 us (44%)
  blocking collectives  34 us (21%)
  starting transfers between devices  26.6 us (16%)
  between operations  13.6 us (8%)
  local copies, waits for them, and re-layouts  11.7 us (7%)
  matrix products  3.54 us (2%)
    all_gather x1, waiting for transfers between devices, body(): rows = lax.all_gather(occupied, WIDE, axis=0, tiled=True)  47.4 us
    all_to_all x1, blocking collectives, body(): got = lax.all_to_all(tiles, PLANE, 0, 0, tiled=True)  34 us
    all_to_all x2, waiting for transfers between devices, exchange(): got = lax.all_to_all(pieces, PLANE, 0, 0, tiled=True)  23 us
    all_to_all x2, starting transfers between devices, exchange(): got = lax.all_to_all(pieces, PLANE, 0, 0, tiled=True)  19.4 us
    all_to_all x1, starting transfers between devices, body(): columns = jnp.concatenate(lax.all_to_all(sent, 'y', 0, 0), axis=0)  7.12 us
  transfers between devices with their start and end apart: 4, of which 3 were waited for; matrix products, arithmetic and copies ran while one was open for 4% of the time, Pallas kernels for 0%

profile of v1, /device:TPU:6, one launch (start us, length us, event | category | flops | bytes accessed | tf_op | source)
XLA Modules:
  0.0 161.3 jit_solution(2917957493650729534)
XLA Ops:
  6.5 0.8 broadcast_compare_fusion
  7.3 1.3 reshape.48
  8.6 0.6 fusion.1
  9.2 0.9 reshape.49
  10.2 13.9 %all-to-all-start = ((bf16[64,16,128]{2,1,0:T(8,128)(2,1)}), bf16[64,16,128]{2,1,0:T(8,128)(2,1)S(1)}, u32[]{:S(2)}, u32[]{:S(2)}) async-start(bf16[64,16,128]{2,1,0:T(8,128)(2,1)} %reshape.49), calls=%async_computation | async-start | bytes 524288 | tf_op jit(solution)/shard_map/all_to_all | solution.py:15
  24.1 0.1 reshape.52
  24.2 0.1 broadcast_in_dim.23
  24.4 0.3 convolution_convert_fusion.2
  24.7 0.3 reshape_reshape.8
  25.0 0.5 copy.36
  25.6 1.0 reshape.53
  26.5 10.4 %all-to-all-done = bf16[64,16,128]{2,1,0:T(8,128)(2,1)S(1)} async-done(((bf16[64,16,128]{2,1,0:T(8,128)(2,1)}), bf16[64,16,128]{2,1,0:T(8,128)(2,1)S(1)}, u32[]{:S(2)}, u32[]{:S(2)}) %all-to-all-start) | async-done | bytes 262176 | tf_op jit(solution)/shard_map/all_to_all | solution.py:15
  36.9 5.5 %all-to-all-start.2 = ((bf16[64,16,128]{2,1,0:T(8,128)(2,1)}), bf16[64,16,128]{2,1,0:T(8,128)(2,1)S(1)}, u32[]{:S(2)}, u32[]{:S(2)}) async-start(bf16[64,16,128]{2,1,0:T(8,128)(2,1)} %reshape.53), calls=%async_computation.2 | async-start | bytes 524288 | tf_op jit(solution)/shard_map/all_to_all | solution.py:15
  42.4 0.0 all-gather.2.cloned.1.call-start
  42.5 0.1 copy.22
  42.5 0.1 copy.37
  42.6 12.6 %all-to-all-done.2 = bf16[64,16,128]{2,1,0:T(8,128)(2,1)S(1)} async-done(((bf16[64,16,128]{2,1,0:T(8,128)(2,1)}), bf16[64,16,128]{2,1,0:T(8,128)(2,1)S(1)}, u32[]{:S(2)}, u32[]{:S(2)}) %all-to-all-start.2) | async-done | bytes 262176 | tf_op jit(solution)/shard_map/all_to_all | solution.py:15
  55.3 0.1 copy.24
  55.3 0.2 reshape_reshape.9
  55.6 0.3 fusion
  55.9 1.2 reshape.55
  57.1 0.0 all-gather.2.cloned.1.call-update
  57.1 1.6 stack.3
  58.7 7.1 %all-to-all-start.1 = ((bf16[8,64,2048]{2,1,0:T(8,128)(2,1)}), bf16[8,64,2048]{2,1,0:T(8,128)(2,1)S(1)}, u32[]{:S(2)}, u32[]{:S(2)}) async-start(bf16[8,64,2048]{2,1,0:T(8,128)(2,1)} %stack.3), calls=%async_computation.1 | async-start | bytes 4194304 | tf_op jit(solution)/shard_map/all_to_all | solution.py:38
  65.8 47.4 %all-gather.2.cloned.1.call-done = bf16[512,2048]{1,0:T(8,128)(2,1)} async-done(((bf16[64,2048]{1,0:T(8,128)(2,1)}), bf16[512,2048]{1,0:T(8,128)(2,1)}) %all-gather.2.cloned.1.call-update) | async-done | bytes 2097168 | tf_op jit(solution)/shard_map/all_gather | solution.py:42
  113.3 3.2 %copy.26 = bf16[4,8,16,2048]{3,2,1,0:T(8,128)(2,1)} copy(bf16[4,8,16,2048]{3,2,0,1:T(8,128)(2,1)} %bitcast.39) | data formatting | bytes 4194304 | tf_op jit(solution)/shard_map/transpose | solution.py:43
  116.4 2.9 %convolution_convert_fusion = bf16[512,512]{1,0:T(8,128)(2,1)S(1)} fusion(bf16[512,2048]{1,0:T(8,128)(2,1)S(1)} %bitcast.40, bf16[512,2048]{1,0:T(8,128)(2,1)} %bitcast.41), kind=kOutput, calls=%fused_computation | convolution fusion | flops 1074003968 | bytes 4718592 | tf_op jit(solution)/shard_map/dot_general | solution.py:44
  119.3 0.1 reshape.58
  119.4 0.1 copy.27
  119.5 34.0 %all_to_all.20 = bf16[64,32,128]{2,1,0:T(8,128)(2,1)S(1)} all-to-all(bf16[64,32,128]{2,1,0:T(8,128)(2,1)S(1)} %bitcast.43), channel_id=1, replica_groups=mesh['x_lo'=2,'y'=8,'core'=2,'z'=8,'x_hi'=2] {'x_lo','core','z','x_hi'}, dimensions={0} | all-to-all | bytes 1048576 | tf_op jit(solution)/shard_map/all_to_all | solution.py:49
  153.6 0.1 convert_reduce_fusion
  153.7 0.8 copy.29
  (9 shorter events, 0.0 us)
Async XLA Ops:
  6.5 17.8 %copy-start = (bf16[512,512]{1,0:T(8,128)(2,1)S(1)}, bf16[512,512]{1,0:T(8,128)(2,1)}, u32[]{:S(2)}) copy-start(bf16[512,512]{1,0:T(8,128)(2,1)} %param.6) | copy-start | bytes 1572868
  6.5 17.5 %copy-start.1 = (bf16[128,2,512]{2,1,0:T(2,128)(2,1)S(1)}, bf16[128,2,512]{2,1,0:T(2,128)(2,1)}, u32[]{:S(2)}) copy-start(bf16[128,2,512]{2,1,0:T(2,128)(2,1)} %param.4) | copy-start | bytes 786436
  10.2 26.8 %all-to-all-start = ((bf16[64,16,128]{2,1,0:T(8,128)(2,1)}), bf16[64,16,128]{2,1,0:T(8,128)(2,1)S(1)}, u32[]{:S(2)}, u32[]{:S(2)}) async-start(bf16[64,16,128]{2,1,0:T(8,128)(2,1)} %reshape.49), calls=%async_computation | async-start | bytes 524288 | tf_op jit(solution)/shard_map/all_to_all | solution.py:15
  25.5 30.0 %copy-start.2 = (bf16[32,32]{1,0:T(8,128)(2,1)S(1)}, bf16[32,32]{1,0:T(8,128)(2,1)}, u32[]{:S(2)}) copy-start(bf16[32,32]{1,0:T(8,128)(2,1)} %param.5) | copy-start | bytes 6148
  36.9 18.3 %all-to-all-start.2 = ((bf16[64,16,128]{2,1,0:T(8,128)(2,1)}), bf16[64,16,128]{2,1,0:T(8,128)(2,1)S(1)}, u32[]{:S(2)}, u32[]{:S(2)}) async-start(bf16[64,16,128]{2,1,0:T(8,128)(2,1)} %reshape.53), calls=%async_computation.2 | async-start | bytes 524288 | tf_op jit(solution)/shard_map/all_to_all | solution.py:15
  42.4 70.8 %all-gather.2.cloned.1.call-start = ((), (), s32[]{:S(2)}) async-start(), calls=%async_computation.4 | async-start | bytes 2359296 | tf_op jit(solution)/shard_map/all_gather | solution.py:42
  58.7 57.7 %all-to-all-start.1 = ((bf16[8,64,2048]{2,1,0:T(8,128)(2,1)}), bf16[8,64,2048]{2,1,0:T(8,128)(2,1)S(1)}, u32[]{:S(2)}, u32[]{:S(2)}) async-start(bf16[8,64,2048]{2,1,0:T(8,128)(2,1)} %stack.3), calls=%async_computation.1 | async-start | bytes 4194304 | tf_op jit(solution)/shard_map/all_to_all | solution.py:38
Sparse Core Ops, SparseCore 0:
  57.2 55.9 all-gather.1
